TPU v7x, 32 devices: a whole 2x2x4 slice. The times are simulated.
32 devices in a mesh: param: 8 (over y, x, core), ex: 4 (over z).
Axes of the slice: x: 2, y: 2, z: 4, core: 2. Of those that a mesh axis runs over, the one named last changes fastest.
Arguments:
- grads: float32 [49152, 2048], P('param', 'ex'), may hold values from -6 to 6
- projection: bfloat16 [49152, 1024], P('param'), may hold values from -6 to 6
- whitener: float32 [1024, 1024], P('param'), may hold values from -1 to 3
Outputs:
- scores: float32 [2048, 2048], P('ex', 'param')
All inputs are finite; a program needn't handle non-finite values.
Results may differ from a plain program's by a relative error of at most 0.0052.
Values may be sent and summed in bfloat16 or wider, within the bound.
A program may use at most 128 MiB of HBM per device.

v0:
```python
import math
import jax
import jax.numpy as jnp
from jax import lax
from jax.sharding import PartitionSpec as P


def body(grads, projection, whitener):
    low_grads = grads.astype(jnp.bfloat16)
    partial_value = lax.dot_general(
        projection, low_grads, (((0,), (0,)), ((), ())), preferred_element_type=jnp.float32
    )
    param_count = lax.axis_size("param")
    ex_count = lax.axis_size("ex")
    norm_factor = 1.0 / math.sqrt(grads.shape[0] * param_count)
    whole_whitener = lax.all_gather(whitener, "param", axis=0, tiled=True)
    sketch_rows = partial_value.shape[0]
    local_width = grads.shape[1]
    total_width = local_width * ex_count
    tile_width = total_width // param_count
    col_start = lax.axis_index("param") * tile_width
    owned_share = (
        lax.psum_scatter(partial_value, "param", scatter_dimension=1, tiled=True) * norm_factor
    )
    whitened = jnp.dot(whole_whitener, owned_share, precision=lax.Precision.HIGHEST).astype(
        jnp.bfloat16
    )
    joined = lax.all_gather(whitened, ("param", "ex"), axis=1, tiled=True)
    piece_width = owned_share.shape[1]
    all_columns = joined.reshape(sketch_rows, param_count, ex_count, piece_width)
    all_columns = all_columns.transpose(0, 2, 1, 3).reshape(
        sketch_rows, param_count * ex_count * piece_width
    )
    row_start = lax.axis_index("ex") * local_width
    row_block = lax.dynamic_slice_in_dim(all_columns, row_start, local_width, 1)
    col_block = lax.dynamic_slice_in_dim(all_columns, col_start, tile_width, 1)
    tile = lax.dot_general(
        row_block, col_block, (((0,), (0,)), ((), ())), preferred_element_type=jnp.float32
    )
    return tile / sketch_rows


def solution(mesh):
    return jax.shard_map(
        body,
        mesh=mesh,
        in_specs=(P("param", "ex"), P("param", None), P("param", None)),
        out_specs=P("ex", "param"),
        check_vma=False,
    )
```

profile of v0, /device:TPU:0, one launch (start us, length us, event | category | flops | bytes accessed | tf_op | source)
XLA Modules:
  0.0 182.8 jit_solution(3519660130798700273)
XLA Ops:
  6.5 0.0 reduce-scatter.4.cloned.1.call-start
  6.5 14.3 %fusion.2 = f32[512,1024]{1,0:T(8,128)} fusion(bf16[6144,1024]{1,0:T(8,128)(2,1)} %param.4, f32[6144,512]{1,0:T(8,128)} %param.3), kind=kOutput, calls=%fused_computation.2 | convolution fusion | flops 6445596672 | bytes 27262976
  20.9 0.0 reduce-scatter.4.cloned.1.call-update
  20.9 0.0 all-gather.3.cloned.1.call-start
  20.9 0.7 all-gather.3.cloned.1.call-update
  21.6 0.0 all-gather.5.cloned.1.call-start
  21.7 43.2 %reduce-scatter.4.cloned.1.call-done = f32[64,1024]{1,0:T(8,128)} async-done(((f32[512,1024]{1,0:T(8,128)}), f32[64,1024]{1,0:T(8,128)}) %reduce-scatter.4.cloned.1.call-update) | async-done | bytes 262160
  64.9 1.1 copy.9
  66.0 37.3 %all-gather.3.cloned.1.call-done = f32[1024,1024]{1,0:T(8,128)} async-done(((f32[128,1024]{1,0:T(8,128)}), f32[1024,1024]{1,0:T(8,128)}) %all-gather.3.cloned.1.call-update) | async-done | bytes 4194320 | tf_op jit(solution)/shard_map/all_gather | solution.py:16
  103.4 7.2 %fusion.5 = bf16[1024,64]{0,1:T(8,128)(2,1)} fusion(f32[1024,1024]{1,0:T(8,128)} %all-gather.3.cloned.1.call-done, f32[1024,64]{1,0:T(8,128)S(1)} %copy.9), kind=kOutput, calls=%fused_computation.5 | convolution fusion | flops 805437440 | bytes 4587520 | tf_op jit(solution)/shard_map/dot_general | solution.py:25
  110.5 0.0 all-gather.5.cloned.1.call-update
  110.6 61.8 %all-gather.5.cloned.1.call-done = bf16[1024,2048]{0,1:T(8,128)(2,1)} async-done(((bf16[1024,64]{0,1:T(8,128)(2,1)}), bf16[1024,2048]{0,1:T(8,128)(2,1)}) %all-gather.5.cloned.1.call-update) | async-done | bytes 4194320 | tf_op jit(solution)/shard_map/all_gather | solution.py:28
  172.3 2.6 %copy.6 = bf16[1024,8,4,64]{0,3,1,2:T(8,128)(2,1)S(1)} copy(bf16[1024,8,4,64]{0,3,2,1:T(8,128)(2,1)} %bitcast.12) | data formatting | bytes 8388608 | tf_op jit(solution)/shard_map/reshape | solution.py:30
  175.0 1.3 convolution_multiply_fusion
Async XLA Ops:
  6.5 58.3 %reduce-scatter.4.cloned.1.call-start = ((), (), s32[]{:S(2)}) async-start(), calls=%async_computation.3 | async-start | bytes 2359296
  20.9 82.5 %all-gather.3.cloned.1.call-start = ((), (), s32[]{:S(2)}) async-start(), calls=%async_computation.1 | async-start | bytes 4718592 | tf_op jit(solution)/shard_map/all_gather | solution.py:16
  21.6 150.7 %all-gather.5.cloned.1.call-start = ((), (), s32[]{:S(2)}) async-start(), calls=%async_computation.2 | async-start | bytes 4325376 | tf_op jit(solution)/shard_map/all_gather | solution.py:28
Sparse Core Ops, SparseCore 0:
  21.0 43.8 reduce-scatter.3
  66.8 36.5 all-gather.2
  110.7 61.6 all-gather.4
where the time goes:
time: 183 us
  waiting for transfers between devices  143 us (78%)
  matrix products  22.8 us (12%)
  between operations  13.1 us (7%)
  local copies, waits for them, and re-layouts  3.77 us (2%)
    all_gather x1, waiting for transfers between devices, body(): joined = lax.all_gather(whitened, ('param', 'ex'), axis=1, tiled=True)  61.8 us
    unnamed x4, waiting for transfers between devices  43.9 us
    all_gather x1, waiting for transfers between devices, body(): whole_whitener = lax.all_gather(whitener, 'param', axis=0, tiled=True)  37.3 us
    unnamed x1, matrix products  14.3 us
    dot_general x1, matrix products, body(): jnp.dot(whole_whitener, owned_share, precision=lax.Precision.HIGHEST)  7.16 us
  transfers between devices with their start and end apart: 3, of which 3 were waited for; matrix products, arithmetic and copies ran while one was open for 1% of the time, Pallas kernels for 0%

commit v1 on v0

--- a/solution.py
+++ b/solution.py
@@ -13,7 +13,14 @@
     param_count = lax.axis_size("param")
     ex_count = lax.axis_size("ex")
     norm_factor = 1.0 / math.sqrt(grads.shape[0] * param_count)
-    whole_whitener = lax.all_gather(whitener, "param", axis=0, tiled=True)
+    ring = [whitener]
+    for hop in range(7):
+        ring.append(lax.ppermute(ring[-1], "param", [(dev, (dev + 1) % 8) for dev in range(8)]))
+    whole_whitener = jnp.roll(
+        jnp.concatenate(ring[::-1], axis=0),
+        (lax.axis_index("param") + 1) * ring[0].shape[0],
+        axis=0,
+    )
     sketch_rows = partial_value.shape[0]
     local_width = grads.shape[1]
     total_width = local_width * ex_count

time: 183 us -> 173 us (0.945)
  waiting for transfers between devices: 143 us -> 127 us
  local copies, waits for them, and re-layouts: 3.77 us -> 10.4 us
  matrix products: 22.8 us -> 20.5 us
  starting transfers between devices: 0.08 us -> 2.06 us
    ppermute x0 -> x7, waiting for transfers between devices: none -> 55.3 us  [body(): lax.ppermute(ring[-1], 'param', [(dev, (dev + 1) % 8) for dev in range(8)])]
    unnamed x4 -> x3, waiting for transfers between devices: 43.9 us -> 4.48 us
    all_gather x1 -> x0, waiting for transfers between devices: 37.3 us -> none  [body(): whole_whitener = lax.all_gather(whitener, 'param', axis=0, tiled=True)]
    unnamed x1 -> x22, local copies, waits for them, and re-layouts: 1.14 us -> 7.71 us
    all_gather x1, waiting for transfers between devices: 61.8 us -> 66.8 us  [body(): joined = lax.all_gather(whitened, ('param', 'ex'), axis=1, tiled=True)]
    dot_general x1, matrix products: 7.16 us -> 4.91 us  [body(): jnp.dot(whole_whitener, owned_share, precision=lax.Precision.HIGHEST)]
    ppermute x0 -> x7, starting transfers between devices: none -> 2.02 us  [body(): lax.ppermute(ring[-1], 'param', [(dev, (dev + 1) % 8) for dev in range(8)])]
  transfers between devices with their start and end apart: 3 -> 9, of which waited for: 3 -> 8; matrix products, arithmetic and copies ran while one was open for 1% -> 9% of each run, Pallas kernels for 0% -> 0%
where the time goes in v1:
time: 173 us
  waiting for transfers between devices  127 us (73%)
  matrix products  20.5 us (12%)
  between operations  13.6 us (8%)
  local copies, waits for them, and re-layouts  10.4 us (6%)
  starting transfers between devices  2.06 us (1%)
    all_gather x1, waiting for transfers between devices, body(): joined = lax.all_gather(whitened, ('param', 'ex'), axis=1, tiled=True)  66.8 us
    ppermute x7, waiting for transfers between devices, body(): lax.ppermute(ring[-1], 'param', [(dev, (dev + 1) % 8) for dev in range(8)])  55.3 us
    unnamed x1, matrix products  14.3 us
    unnamed x22, local copies, waits for them, and re-layouts  7.71 us
    dot_general x1, matrix products, body(): jnp.dot(whole_whitener, owned_share, precision=lax.Precision.HIGHEST)  4.91 us
    unnamed x3, waiting for transfers between devices  4.48 us
  transfers between devices with their start and end apart: 9, of which 8 were waited for; matrix products, arithmetic and copies ran while one was open for 9% of the time, Pallas kernels for 0%

profile of v1, /device:TPU:0, one launch (start us, length us, event | category | flops | bytes accessed | tf_op | source)
XLA Modules:
  0.0 173.1 jit_solution(5415028639301929488)
XLA Ops:
  6.5 0.0 reduce-scatter.4.cloned.1.call-start
  6.5 0.5 collective-permute-start
  7.0 9.9 %collective-permute-done = f32[128,1024]{1,0:T(8,128)S(1)} collective-permute-done((f32[128,1024]{1,0:T(8,128)}, f32[128,1024]{1,0:T(8,128)S(1)}, u32[]{:S(2)}, u32[]{:S(2)}) %collective-permute-start) | collective-permute-done | bytes 524320 | tf_op jit(solution)/shard_map/ppermute | solution.py:18
  17.0 0.0 collective-permute-start.1
  17.0 14.3 %fusion.4 = f32[512,1024]{1,0:T(8,128)} fusion(bf16[6144,1024]{1,0:T(8,128)(2,1)} %param.4, f32[6144,512]{1,0:T(8,128)} %param.3), kind=kOutput, calls=%fused_computation.4 | convolution fusion | flops 6445596672 | bytes 27262976
  31.3 0.0 copy-start
  31.3 0.0 reduce-scatter.4.cloned.1.call-update
  31.3 0.0 all-gather.2.cloned.1.call-start
  31.4 0.0 collective-permute-done.1
  31.4 1.5 collective-permute-start.2
  32.9 8.0 %collective-permute-done.2 = f32[128,1024]{1,0:T(8,128)S(1)} collective-permute-done((f32[128,1024]{1,0:T(8,128)S(1)}, f32[128,1024]{1,0:T(8,128)S(1)}, u32[]{:S(2)}, u32[]{:S(2)}) %collective-permute-start.2) | collective-permute-done | bytes 524320 | tf_op jit(solution)/shard_map/ppermute | solution.py:18
  40.9 0.0 collective-permute-start.3
  40.9 9.5 %collective-permute-done.3 = f32[128,1024]{1,0:T(8,128)S(1)} collective-permute-done((f32[128,1024]{1,0:T(8,128)S(1)}, f32[128,1024]{1,0:T(8,128)S(1)}, u32[]{:S(2)}, u32[]{:S(2)}) %collective-permute-start.3) | collective-permute-done | bytes 524320 | tf_op jit(solution)/shard_map/ppermute | solution.py:18
  50.4 0.0 collective-permute-start.4
  50.5 13.9 %collective-permute-done.4 = f32[128,1024]{1,0:T(8,128)S(1)} collective-permute-done((f32[128,1024]{1,0:T(8,128)S(1)}, f32[128,1024]{1,0:T(8,128)S(1)}, u32[]{:S(2)}, u32[]{:S(2)}) %collective-permute-start.4) | collective-permute-done | bytes 524320 | tf_op jit(solution)/shard_map/ppermute | solution.py:18
  64.4 0.0 copy-start.1
  64.4 0.8 copy-done.1
  65.2 0.0 collective-permute-start.5
  65.2 9.7 %collective-permute-done.5 = f32[128,1024]{1,0:T(8,128)} collective-permute-done((f32[128,1024]{1,0:T(8,128)S(1)}, f32[128,1024]{1,0:T(8,128)}, u32[]{:S(2)}, u32[]{:S(2)}) %collective-permute-start.5) | collective-permute-done | bytes 524320 | tf_op jit(solution)/shard_map/ppermute | solution.py:18
  74.9 0.0 collective-permute-start.6
  74.9 4.4 %reduce-scatter.4.cloned.1.call-done = f32[64,1024]{1,0:T(8,128)} async-done(((f32[512,1024]{1,0:T(8,128)}), f32[64,1024]{1,0:T(8,128)}) %reduce-scatter.4.cloned.1.call-update) | async-done | bytes 262160
  79.3 1.1 copy.9
  80.5 0.0 copy-start.2
  80.5 4.2 %collective-permute-done.6 = f32[128,1024]{1,0:T(8,128)} collective-permute-done((f32[128,1024]{1,0:T(8,128)}, f32[128,1024]{1,0:T(8,128)}, u32[]{:S(2)}, u32[]{:S(2)}) %collective-permute-start.6) | collective-permute-done | bytes 524320 | tf_op jit(solution)/shard_map/ppermute | solution.py:18
  84.7 1.1 constant_dynamic-update-slice_fusion.15
  85.8 1.1 constant_dynamic-update-slice_fusion.14
  86.9 1.1 constant_dynamic-update-slice_fusion.13
  88.1 0.0 copy-done
  88.2 1.1 constant_dynamic-update-slice_fusion.7
  89.3 1.1 constant_dynamic-update-slice_fusion.6
  90.3 0.0 copy-done.2
  90.6 4.9 %fusion.7 = bf16[1024,64]{0,1:T(8,128)(2,1)} fusion(f32[2048,1024]{1,0:T(8,128)S(1)} %constant_dynamic-update-slice_fusion, s32[]{:T(128)S(6)} %select_n.20, f32[1024,64]{1,0:T(8,128)S(1)} %copy.9), kind=kOutput, calls=%fused_computation.6 | convolution fusion | flops 805437440 | bytes 4849668 | tf_op jit(solution)/shard_map/dot_general | solution.py:32
  95.5 0.0 all-gather.2.cloned.1.call-update
  95.6 66.8 %all-gather.2.cloned.1.call-done = bf16[1024,2048]{0,1:T(8,128)(2,1)} async-done(((bf16[1024,64]{0,1:T(8,128)(2,1)}), bf16[1024,2048]{0,1:T(8,128)(2,1)}) %all-gather.2.cloned.1.call-update) | async-done | bytes 4194320 | tf_op jit(solution)/shard_map/all_gather | solution.py:35
  162.3 2.6 %copy.6 = bf16[1024,8,4,64]{0,3,1,2:T(8,128)(2,1)S(1)} copy(bf16[1024,8,4,64]{0,3,2,1:T(8,128)(2,1)} %bitcast.9) | data formatting | bytes 8388608 | tf_op jit(solution)/shard_map/reshape | solution.py:37
  165.0 1.3 convolution_multiply_fusion
  (11 shorter events, 0.4 us)
Async XLA Ops:
  6.5 72.8 %reduce-scatter.4.cloned.1.call-start = ((), (), s32[]{:S(2)}) async-start(), calls=%async_computation.2 | async-start | bytes 2359296
  6.5 10.4 %collective-permute-start = (f32[128,1024]{1,0:T(8,128)}, f32[128,1024]{1,0:T(8,128)S(1)}, u32[]{:S(2)}, u32[]{:S(2)}) collective-permute-start(f32[128,1024]{1,0:T(8,128)} %param.5), channel_id=1, source_target_pairs={{0,4},{4,8},{8,12},{12,16},{16,20},{20,24},{24,28},{28,0},{1,5},{5... | collective-permute-start | bytes 1572872 | tf_op jit(solution)/shard_map/ppermute | solution.py:18
  17.0 14.4 %collective-permute-start.1 = (f32[128,1024]{1,0:T(8,128)S(1)}, f32[128,1024]{1,0:T(8,128)S(1)}, u32[]{:S(2)}, u32[]{:S(2)}) collective-permute-start(f32[128,1024]{1,0:T(8,128)S(1)} %collective-permute-done), channel_id=1, source_target_pairs={{0,4},{4,8},{8,12},{12,16},{16,20},{20,24},{24,28},{28,0},{1,5},{5... | collective-permute-start | bytes 1572872 | tf_op jit(solution)/shard_map/ppermute | solution.py:18
  31.3 56.8 %copy-start = (f32[128,1024]{1,0:T(8,128)S(1)}, f32[128,1024]{1,0:T(8,128)}, u32[]{:S(2)}) copy-start(f32[128,1024]{1,0:T(8,128)} %param.5) | copy-start | bytes 1572868
  31.3 131.0 %all-gather.2.cloned.1.call-start = ((), (), s32[]{:S(2)}) async-start(), calls=%async_computation.1 | async-start | bytes 4325376 | tf_op jit(solution)/shard_map/all_gather | solution.py:35
  31.4 9.6 %collective-permute-start.2 = (f32[128,1024]{1,0:T(8,128)S(1)}, f32[128,1024]{1,0:T(8,128)S(1)}, u32[]{:S(2)}, u32[]{:S(2)}) collective-permute-start(f32[128,1024]{1,0:T(8,128)S(1)} %collective-permute-done.1), channel_id=1, source_target_pairs={{0,4},{4,8},{8,12},{12,16},{16,20},{20,24},{24,28},{28,0},{1,5},{5... | collective-permute-start | bytes 1572872 | tf_op jit(solution)/shard_map/ppermute | solution.py:18
  40.9 9.5 %collective-permute-start.3 = (f32[128,1024]{1,0:T(8,128)S(1)}, f32[128,1024]{1,0:T(8,128)S(1)}, u32[]{:S(2)}, u32[]{:S(2)}) collective-permute-start(f32[128,1024]{1,0:T(8,128)S(1)} %collective-permute-done.2), channel_id=1, source_target_pairs={{0,4},{4,8},{8,12},{12,16},{16,20},{20,24},{24,28},{28,0},{1,5},{5... | collective-permute-start | bytes 1572872 | tf_op jit(solution)/shard_map/ppermute | solution.py:18
  50.4 13.9 %collective-permute-start.4 = (f32[128,1024]{1,0:T(8,128)S(1)}, f32[128,1024]{1,0:T(8,128)S(1)}, u32[]{:S(2)}, u32[]{:S(2)}) collective-permute-start(f32[128,1024]{1,0:T(8,128)S(1)} %collective-permute-done.3), channel_id=1, source_target_pairs={{0,4},{4,8},{8,12},{12,16},{16,20},{20,24},{24,28},{28,0},{1,5},{5... | collective-permute-start | bytes 1572872 | tf_op jit(solution)/shard_map/ppermute | solution.py:18
  64.4 0.8 copy-start.1
  65.2 9.7 %collective-permute-start.5 = (f32[128,1024]{1,0:T(8,128)S(1)}, f32[128,1024]{1,0:T(8,128)}, u32[]{:S(2)}, u32[]{:S(2)}) collective-permute-start(f32[128,1024]{1,0:T(8,128)S(1)} %collective-permute-done.4), channel_id=1, source_target_pairs={{0,4},{4,8},{8,12},{12,16},{16,20},{20,24},{24,28},{28,0},{1,5},{5... | collective-permute-start | bytes 1572872 | tf_op jit(solution)/shard_map/ppermute | solution.py:18
  74.9 9.8 %collective-permute-start.6 = (f32[128,1024]{1,0:T(8,128)}, f32[128,1024]{1,0:T(8,128)}, u32[]{:S(2)}, u32[]{:S(2)}) collective-permute-start(f32[128,1024]{1,0:T(8,128)} %collective-permute-done.5), channel_id=1, source_target_pairs={{0,4},{4,8},{8,12},{12,16},{16,20},{20,24},{24,28},{28,0},{1,5},{5... | collective-permute-start | bytes 1572872 | tf_op jit(solution)/shard_map/ppermute | solution.py:18
  80.5 9.9 %copy-start.2 = (f32[128,1024]{1,0:T(8,128)S(1)}, f32[128,1024]{1,0:T(8,128)}, u32[]{:S(2)}) copy-start(f32[128,1024]{1,0:T(8,128)} %copy-done.1) | copy-start | bytes 1572868
Sparse Core Ops, SparseCore 0:
  31.4 47.8 reduce-scatter.3
  95.7 66.6 all-gather.1
